TPU v7x, 32 devices: a whole 2x2x4 slice. The times are simulated.
32 devices in a mesh: face: 8 (over z, x), band: 4 (over y, core).
Axes of the slice: x: 2, y: 2, z: 4, core: 2. Of those that a mesh axis runs over, the one named last changes fastest.
Arguments:
- node_latents: bfloat16 [8192, 512], P(('face', 'band')), may hold values from -6 to 6
- coarse_latents: bfloat16 [1024, 512], replicated, may hold values from -6 to 6
- edge_latents: bfloat16 [32768, 512], P(('face', 'band')), may hold values from -6 to 6
- up_latents: bfloat16 [8192, 512], P(('face', 'band')), may hold values from -6 to 6
- edge_weight_in: bfloat16 [1536, 512], replicated, may hold values from -0.15625 to 0.15625
- edge_weight_out: bfloat16 [512, 512], replicated, may hold values from -0.25 to 0.25
- edge_gain: float32 [512], replicated, may hold values from 0.5 to 1.5
- node_weight_in: bfloat16 [1024, 512], replicated, may hold values from -0.1875 to 0.1875
- node_weight_out: bfloat16 [512, 512], replicated, may hold values from -0.25 to 0.25
- node_gain: float32 [512], replicated, may hold values from 0.5 to 1.5
- nodes_cotangent: bfloat16 [8192, 512], P(('face', 'band')), may hold values from -6 to 6
- coarse_cotangent: bfloat16 [1024, 512], replicated, may hold values from -6 to 6
- edges_cotangent: bfloat16 [32768, 512], P(('face', 'band')), may hold values from -6 to 6
- ups_cotangent: bfloat16 [8192, 512], P(('face', 'band')), may hold values from -6 to 6
- send_rows: int32 [32, 32, 4], P(('face', 'band')), may hold values from 0 to 255, as said below
- edge_sender: int32 [32768], P(('face', 'band')), may hold values from 0 to 1407, as said below
- edge_receiver: int32 [32768], P(('face', 'band')), may hold values from 0 to 255
- up_sender: int32 [8192], P(('face', 'band')), may hold values from 0 to 255
- up_receiver: int32 [8192], P(('face', 'band')), may hold values from 0 to 1023
Outputs:
- grad_nodes: float32 [8192, 512], P(('face', 'band'))
- grad_coarse: float32 [1024, 512], replicated
- grad_edges: float32 [32768, 512], P(('face', 'band'))
- grad_ups: float32 [8192, 512], P(('face', 'band'))
- grad_edge_in: float32 [1536, 512], replicated
- grad_edge_out: float32 [512, 512], replicated
- grad_edge_gain: float32 [512], replicated
- grad_node_in: float32 [1024, 512], replicated
- grad_node_out: float32 [512, 512], replicated
- grad_node_gain: float32 [512], replicated
Inputs may be any that keep to these rules, and one draw needn't show every extreme that they name: `send_rows`: entry [s, p, k] is a row of device s's nodes sent to device p in slot k. Each pair uses its first few slots, at most 4; every device fills all 4 slots to at least one device, and in every draw some device receives 4 rows from every device. Unused slots hold 0 and no edge reads them. `edge_sender`: an edge of device p reads row t of p's sender table: its own node t below 256; slot k of the rows that device s sends to p for t = 256 + s * 4 + k, always a used slot; coarse node t - 384 from 384 on.
All inputs are finite; a program needn't handle non-finite values.
Results may differ from a plain program's by a relative error of at most 0.0068.
Values may be sent and summed in bfloat16 or wider, within the bound.
No kernel may reach another device: no remote copies, remote signals or barrier semaphores. Data moves between devices by JAX's collectives and lax.ppermute only.
A program may use at most 192 MiB of HBM per device.

v0:
```python
import math
import jax
import jax.numpy as jnp
from jax import lax
from jax.sharding import PartitionSpec as P

EPSILON = 1e-05


def mlp_forward(inputs, residual_base, first_weight, second_weight, gain_vec):
    pre_act = jnp.dot(inputs, first_weight, preferred_element_type=jnp.float32)
    hidden_act = jax.nn.silu(pre_act).astype(jnp.bfloat16)
    projected = jnp.dot(hidden_act, second_weight, preferred_element_type=jnp.float32)
    center = projected - jnp.mean(projected, axis=1, keepdims=True)
    inv_std = lax.rsqrt(jnp.mean(center * center, axis=1, keepdims=True) + EPSILON)
    normed = center * inv_std
    return (residual_base + normed * gain_vec, (pre_act, hidden_act, normed, inv_std))


def mlp_backward(inputs, first_weight, second_weight, gain_vec, cache_vals, cotangent):
    pre_act, hidden_act, normed, inv_std = cache_vals
    grad_gain = jnp.sum(cotangent * normed, axis=0)
    scaled = cotangent * gain_vec
    grad_proj = inv_std * (
        scaled
        - jnp.mean(scaled, axis=1, keepdims=True)
        - normed * jnp.mean(scaled * normed, axis=1, keepdims=True)
    )
    grad_proj = grad_proj.astype(jnp.bfloat16)
    grad_second = jnp.dot(hidden_act.T, grad_proj, preferred_element_type=jnp.float32)
    grad_hidden = jnp.dot(grad_proj, second_weight.T, preferred_element_type=jnp.float32)
    logistic = jax.nn.sigmoid(pre_act)
    grad_pre = (grad_hidden * logistic * (1.0 + pre_act * (1.0 - logistic))).astype(jnp.bfloat16)
    grad_first = jnp.dot(inputs.T, grad_pre, preferred_element_type=jnp.float32)
    grad_inputs = jnp.dot(grad_pre, first_weight.T, preferred_element_type=jnp.float32)
    return (grad_inputs, grad_first, grad_second, grad_gain)


def per_device(
    node_latents,
    coarse_latents,
    edge_latents,
    up_latents,
    edge_weight_in,
    edge_weight_out,
    edge_gain,
    node_weight_in,
    node_weight_out,
    node_gain,
    nodes_cotangent,
    coarse_cotangent,
    edges_cotangent,
    ups_cotangent,
    send_rows,
    edge_sender,
    edge_receiver,
    up_sender,
    up_receiver,
):
    latent_width = node_latents.shape[1]
    node_count = node_latents.shape[0]
    coarse_count = coarse_latents.shape[0]
    devices = lax.axis_size(("face", "band"))
    slot_count = send_rows.shape[2]
    import_count = devices * slot_count
    send_table = send_rows[0]
    outgoing = jnp.take(node_latents, send_table, axis=0)
    face_count = lax.axis_size("face")
    sectioned = outgoing.reshape(face_count, devices // face_count, slot_count, latent_width)
    incoming = lax.all_to_all(
        lax.all_to_all(sectioned, "face", split_axis=0, concat_axis=0, tiled=True),
        "band",
        split_axis=1,
        concat_axis=1,
        tiled=True,
    )
    sender_table = jnp.concatenate(
        [node_latents, incoming.reshape(import_count, latent_width), coarse_latents], 0
    )
    edge_inputs = jnp.concatenate(
        [
            edge_latents,
            jnp.take(sender_table, edge_sender, axis=0),
            jnp.take(node_latents, edge_receiver, axis=0),
        ],
        1,
    )
    edge_output, edge_cache = mlp_forward(
        edge_inputs, edge_latents.astype(jnp.float32), edge_weight_in, edge_weight_out, edge_gain
    )
    new_edges = edge_output.astype(jnp.bfloat16)
    receiver_onehot = (
        jnp.arange(node_count, dtype=jnp.int32)[:, None] == edge_receiver[None, :]
    ).astype(jnp.bfloat16)
    fine_total = jnp.dot(receiver_onehot, new_edges, preferred_element_type=jnp.float32)
    up_inputs = jnp.concatenate(
        [
            up_latents,
            jnp.take(node_latents, up_sender, axis=0),
            jnp.take(coarse_latents, up_receiver, axis=0),
        ],
        1,
    )
    up_output, up_cache = mlp_forward(
        up_inputs, up_latents.astype(jnp.float32), edge_weight_in, edge_weight_out, edge_gain
    )
    new_ups = up_output.astype(jnp.bfloat16)
    node_inputs = jnp.concatenate([node_latents, fine_total.astype(jnp.bfloat16)], 1)
    unused_node, node_cache = mlp_forward(
        node_inputs, node_latents.astype(jnp.float32), node_weight_in, node_weight_out, node_gain
    )
    node_grad_inputs, node_first, node_second, node_gain_grad = mlp_backward(
        node_inputs,
        node_weight_in,
        node_weight_out,
        node_gain,
        node_cache,
        nodes_cotangent.astype(jnp.float32),
    )
    row_ids = jnp.arange(coarse_count, dtype=jnp.int32)
    onehot_rows = (row_ids[:, None] == up_receiver[None, :]).astype(jnp.bfloat16)
    coarse_total = lax.psum(
        jnp.dot(onehot_rows, new_ups, preferred_element_type=jnp.float32), ("face", "band")
    )
    coarse_inputs = jnp.concatenate([coarse_latents, coarse_total.astype(jnp.bfloat16)], 1)
    unused_coarse, coarse_cache = mlp_forward(
        coarse_inputs,
        coarse_latents.astype(jnp.float32),
        node_weight_in,
        node_weight_out,
        node_gain,
    )
    coarse_grad_inputs, coarse_first, coarse_second, coarse_gain_grad = mlp_backward(
        coarse_inputs,
        node_weight_in,
        node_weight_out,
        node_gain,
        coarse_cache,
        coarse_cotangent.astype(jnp.float32),
    )
    coarse_grad = coarse_grad_inputs[:, latent_width:]
    coarse_after = coarse_cotangent.astype(jnp.float32) + coarse_grad_inputs[:, :latent_width]
    node_first_total, node_second_total, node_gain_total = (node_first, node_second, node_gain_grad)
    extra_first, extra_second, extra_gain = (coarse_first, coarse_second, coarse_gain_grad)
    up_cotangent = ups_cotangent.astype(jnp.float32) + jnp.take(coarse_grad, up_receiver, axis=0)
    up_grad_inputs, up_first, up_second, up_gain_grad = mlp_backward(
        up_inputs, edge_weight_in, edge_weight_out, edge_gain, up_cache, up_cotangent
    )
    grad_ups = up_cotangent + up_grad_inputs[:, :latent_width]
    fine_grad = node_grad_inputs[:, latent_width:]
    edge_cotangent = edges_cotangent.astype(jnp.float32) + jnp.take(
        fine_grad, edge_receiver, axis=0
    )
    edge_grad_inputs, edge_first, edge_second, edge_gain_grad = mlp_backward(
        edge_inputs, edge_weight_in, edge_weight_out, edge_gain, edge_cache, edge_cotangent
    )
    grad_edges = edge_cotangent + edge_grad_inputs[:, :latent_width]
    table_grad = jax.ops.segment_sum(
        edge_grad_inputs[:, latent_width : 2 * latent_width],
        edge_sender,
        num_segments=node_count + import_count + coarse_count,
    )
    returning = table_grad[node_count : node_count + import_count].reshape(
        devices, slot_count, latent_width
    )
    face_count = lax.axis_size("face")
    sectioned_back = returning.reshape(face_count, devices // face_count, slot_count, latent_width)
    returned = lax.all_to_all(
        lax.all_to_all(
            sectioned_back.astype(jnp.bfloat16), "face", split_axis=0, concat_axis=0, tiled=True
        ),
        "band",
        split_axis=1,
        concat_axis=1,
        tiled=True,
    ).astype(sectioned_back.dtype)
    grad_nodes = (
        nodes_cotangent.astype(jnp.float32)
        + node_grad_inputs[:, :latent_width]
        + table_grad[:node_count]
        + jax.ops.segment_sum(
            edge_grad_inputs[:, 2 * latent_width :], edge_receiver, num_segments=node_count
        )
        + jax.ops.segment_sum(
            up_grad_inputs[:, latent_width : 2 * latent_width], up_sender, num_segments=node_count
        )
        + jax.ops.segment_sum(
            returned.reshape(import_count, latent_width),
            send_table.reshape(import_count),
            num_segments=node_count,
        )
    )
    coarse_local = table_grad[node_count + import_count :] + jax.ops.segment_sum(
        up_grad_inputs[:, 2 * latent_width :], up_receiver, num_segments=coarse_count
    )
    edge_first_total = edge_first + up_first
    edge_second_total = edge_second + up_second
    edge_gain_total = edge_gain_grad + up_gain_grad
    summed = lax.psum(
        (
            node_first_total,
            node_second_total,
            node_gain_total,
            coarse_local,
            edge_first_total,
            edge_second_total,
            edge_gain_total,
        ),
        ("face", "band"),
    )
    node_summed = (summed[0], summed[1], summed[2])
    edge_summed = (summed[3], summed[4], summed[5], summed[6])
    edge_rows_total = (edge_latents.shape[0] + up_latents.shape[0]) * devices
    node_rows_total = node_count * devices + coarse_count
    edge_scale = 1.0 / math.sqrt(edge_rows_total)
    node_scale = 1.0 / math.sqrt(node_rows_total)
    grad_coarse = edge_summed[0] + coarse_after
    return (
        grad_nodes,
        grad_coarse,
        grad_edges,
        grad_ups,
        edge_summed[1] * edge_scale,
        edge_summed[2] * edge_scale,
        edge_summed[3] * edge_scale,
        (node_summed[0] + extra_first) * node_scale,
        (node_summed[1] + extra_second) * node_scale,
        (node_summed[2] + extra_gain) * node_scale,
    )


def solution(mesh):
    return jax.shard_map(
        per_device,
        mesh=mesh,
        in_specs=(
            P(("face", "band"), None),
            P(),
            P(("face", "band"), None),
            P(("face", "band"), None),
            P(),
            P(),
            P(),
            P(),
            P(),
            P(),
            P(("face", "band"), None),
            P(),
            P(("face", "band"), None),
            P(("face", "band"), None),
            P(("face", "band"), None, None),
            P(("face", "band")),
            P(("face", "band")),
            P(("face", "band")),
            P(("face", "band")),
        ),
        out_specs=(
            P(("face", "band"), None),
            P(),
            P(("face", "band"), None),
            P(("face", "band"), None),
            P(),
            P(),
            P(),
            P(),
            P(),
            P(),
        ),
        check_vma=False,
    )
```

profile of v0, /device:TPU:0, one launch (start us, length us, event | category | flops | bytes accessed | tf_op | source)
XLA Modules:
  0.0 416.2 jit_solution(11921928592498029254)
XLA Ops:
  9.2 1.9 gather_fusion
  11.9 7.3 %all-to-all-start = ((bf16[8,4,4,512]{3,2,1,0:T(4,128)(2,1)}), bf16[8,4,4,512]{3,2,1,0:T(4,128)(2,1)}, u32[]{:S(2)}, u32[]{:S(2)}) async-start(bf16[8,4,4,512]{3,2,1,0:T(4,128)(2,1)} %broadcast_select_fusion.4), calls=%async_computation | async-start | bytes 262144 | tf_op jit(solution)/shard_map/all_to_all | solution.py:71
  24.5 1.6 fusion.40
  27.3 1.9 fusion.22
  29.2 61.8 %all-reduce.6 = bf16[1024,512]{1,0:T(8,128)(2,1)} all-reduce(f32[1024,512]{1,0:T(8,128)} %fusion.22), channel_id=1, replica_groups=mesh['face'=8,'band'=4] {'face','band'}, use_global_device_ids=true, to_apply=%region_12.13 | all-reduce | flops 524288 | bytes 3145728 | tf_op jit(solution)/shard_map/psum | solution.py:122
  91.0 2.8 fusion.15
  93.9 2.2 fusion.66
  96.0 3.0 copy.111
  99.0 2.1 multiply_reduce_fusion.1
  101.2 1.6 fusion.8
  107.2 2.0 copy-done.13
  109.3 1.5 slice.72
  110.8 2.8 gather_fusion.6
  116.7 1.8 fusion.70
  119.0 1.6 copy.104
  120.6 3.3 all-to-all-start.1
  126.5 4.0 gather_fusion.2
  131.7 2.3 copy.109
  136.1 5.1 %gather_fusion.1 = bf16[1024,512]{1,0:T(8,128)(2,1)} fusion(bf16[1408,512]{1,0:T(8,128)(2,1)S(1)} %pad_maximum_fusion.2, s32[1024]{0:T(1024)S(1)} %fusion.45), kind=kCustom, calls=%fused_computation.1 | custom fusion | bytes 2101248 | tf_op jit(solution)/shard_map/jit(_take)/gather | solution.py:83
  141.2 2.4 copy.106
  145.1 1.8 fusion.17
  155.0 1.8 fusion.38
  156.8 4.9 %gather_fusion.3 = f32[1024,512]{1,0:T(8,128)} fusion(f32[256,512]{1,0:T(8,128)S(1)} %slice.68, s32[1024]{0:T(1024)S(1)} %fusion.46), kind=kCustom, calls=%fused_computation.3 | custom fusion | bytes 4198400 | tf_op jit(solution)/shard_map/jit(_take)/gather | solution.py:151
  161.6 3.1 copy.110
  164.8 3.3 multiply_reduce_fusion
  172.5 1.8 fusion.16
  174.3 4.5 %fusion.68 = f32[1024,1536]{1,0:T(8,128)} fusion(bf16[1024,512]{1,0:T(8,128)(2,1)S(1)} %multiply_convert_fusion.2, bf16[1536,512]{1,0:T(8,128)(2,1)S(1)} %copy-done), kind=kOutput, calls=%fused_computation.170 | convolution fusion | flops 1610612736 | bytes 8912896 | tf_op jit(solution)/shard_map/dot_general | solution.py:35
  178.8 2.3 convolution_add_fusion
  181.1 1.7 convolution_add_fusion.2
  182.9 9.1 %scatter_custom_fusion = f32[1408,512]{1,0:T(8,128)} fusion(s32[1024]{0:T(1024)} %param.34, f32[1024,1536]{1,0:T(8,128)} %fusion.68, f32[]{:T(128)} %constant.129.clone.1), kind=kCustom, calls=%fused_computation.28 | custom fusion | flops 524288 | bytes 4981248 | tf_op jit(solution)/shard_map/scatter-add | solution.py:158
  192.0 3.2 slice.75
  195.2 5.1 %scatter_custom_fusion.4 = f32[1024,512]{1,0:T(8,128)} fusion(f32[1024,512]{1,0:T(8,128)} %slice.75, s32[256]{0:T(256)} %param.37, f32[256,1536]{1,0:T(8,128)S(1)} %copy-done.11), kind=kCustom, calls=%fused_computation.83 | custom fusion | flops 131072 | bytes 2621440 | tf_op jit(solution)/shard_map/scatter-add | solution.py:193
  201.1 3.2 scatter_custom_fusion.2
  204.4 1.9 slice_add_fusion
  208.1 4.6 %all-to-all-start.2 = ((bf16[8,4,4,512]{3,2,1,0:T(4,128)(2,1)}), bf16[8,4,4,512]{3,2,1,0:T(4,128)(2,1)S(1)}, u32[]{:S(2)}, u32[]{:S(2)}) async-start(bf16[8,4,4,512]{3,2,1,0:T(4,128)(2,1)} %convert_element_type.97), calls=%async_computation.2 | async-start | bytes 262144 | tf_op jit(solution)/shard_map/all_to_all | solution.py:169
  214.1 42.8 %all-reduce = (f32[512]{0:T(512)S(1)}, f32[512]{0:T(512)S(1)}) all-reduce(f32[512]{0:T(512)S(1)} %add.244, f32[512]{0:T(512)S(1)} %copy-done.51), channel_id=1, replica_groups=mesh['face'=8,'band'=4] {'face','band'}, use_global_device_ids=true, to_apply=%region_27.28 | all-reduce | flops 1024 | bytes 8192 | tf_op jit(solution)/shard_map/psum | solution.py:199
  258.2 3.5 all-to-all-start.3
  262.3 3.3 slice.78
  265.6 2.9 copy.118
  268.5 4.1 add.240
  272.6 2.9 copy.117
  275.5 7.6 %scatter_custom_fusion.1 = f32[256,512]{1,0:T(8,128)S(1)} fusion(f32[256,512]{1,0:T(8,128)S(1)} %fusion.30, s32[1024]{0:T(1024)S(1)} %copy-done.48, f32[1024,1536]{1,0:T(8,128)} %fusion.68), kind=kCustom, calls=%fused_computation.26 | custom fusion | flops 524288 | bytes 2621440 | tf_op jit(solution)/shard_map/scatter-add | solution.py:181
  283.6 1.6 scatter_fusion
  285.1 111.2 %all-reduce.5.cloned.1.call-done = (f32[1024,512]{1,0:T(8,128)}, f32[1536,512]{1,0:T(8,128)}, f32[512,512]{1,0:T(8,128)}, f32[1024,512]{1,0:T(8,128)}, f32[512,512]{1,0:T(8,128)}) async-done(((f32[1024,512]{1,0:T(8,128)}, f32[1536,512]{1,0:T(8,128)}, f32[512,512]{1,0:T(8,128)}, f32[1024,512]{1,0:T(8,128)}, f32[512,512]{1,0:T(8,128)}), (f32[1024,512]{1,0:T(8,128)}, f32[1536,512]{1,0:T(8,128)}, ...) | async-done | bytes 9437200 | tf_op jit(solution)/shard_map/psum | solution.py:199
  396.3 3.8 fusion.14
  400.1 2.6 add_multiply_fusion
  404.1 1.9 fusion.7
  407.0 2.0 broadcast_multiply_fusion
  (229 shorter events, 45.5 us)
Async XLA Ops:
  7.2 17.3 %copy-start = (bf16[1536,512]{1,0:T(8,128)(2,1)S(1)}, bf16[1536,512]{1,0:T(8,128)(2,1)}, u32[]{:S(2)}) copy-start(bf16[1536,512]{1,0:T(8,128)(2,1)} %param.23) | copy-start | bytes 4718596
  7.2 14.7 %copy-start.1 = (bf16[256,512]{1,0:T(8,128)(2,1)S(1)}, bf16[256,512]{1,0:T(8,128)(2,1)}, u32[]{:S(2)}) copy-start(bf16[256,512]{1,0:T(8,128)(2,1)} %param.19) | copy-start | bytes 786436
  11.0 12.1 %copy-start.9 = (bf16[1024,512]{1,0:T(8,128)(2,1)S(1)}, bf16[1024,512]{1,0:T(8,128)(2,1)}, u32[]{:S(2)}) copy-start(bf16[1024,512]{1,0:T(8,128)(2,1)} %param.20) | copy-start | bytes 3145732
  11.9 107.2 %all-to-all-start = ((bf16[8,4,4,512]{3,2,1,0:T(4,128)(2,1)}), bf16[8,4,4,512]{3,2,1,0:T(4,128)(2,1)}, u32[]{:S(2)}, u32[]{:S(2)}) async-start(bf16[8,4,4,512]{3,2,1,0:T(4,128)(2,1)} %broadcast_select_fusion.4), calls=%async_computation | async-start | bytes 262144 | tf_op jit(solution)/shard_map/all_to_all | solution.py:71
  24.5 2.1 copy-start.26
  91.0 2.8 copy-start.56
  93.8 2.2 copy-start.68
  96.0 5.1 %copy-start.7 = (bf16[1024,512]{1,0:T(8,128)(2,1)S(1)}, bf16[1024,512]{1,0:T(8,128)(2,1)}, u32[]{:S(2)}) copy-start(bf16[1024,512]{1,0:T(8,128)(2,1)} %param.30) | copy-start | bytes 3145732
  99.0 2.2 copy-start.2
  99.0 2.2 copy-start.44
  102.8 1.9 copy-start.69
  107.2 2.0 copy-start.13
  110.8 2.9 copy-start.42
  116.7 2.3 copy-start.46
  116.7 8.4 %copy-start.28 = (bf16[1024,512]{1,0:T(8,128)(2,1)S(1)}, bf16[1024,512]{1,0:T(8,128)(2,1)}, u32[]{:S(2)}) copy-start(bf16[1024,512]{1,0:T(8,128)(2,1)} %param.21) | copy-start | bytes 3145732
  120.6 13.4 %all-to-all-start.1 = ((bf16[8,4,4,512]{3,2,0,1:T(4,128)(2,1)}), bf16[8,4,4,512]{3,2,0,1:T(4,128)(2,1)S(1)}, u32[]{:S(2)}, u32[]{:S(2)}) async-start(bf16[8,4,4,512]{3,2,0,1:T(4,128)(2,1)} %copy.104), calls=%async_computation.1 | async-start | bytes 262144 | tf_op jit(solution)/shard_map/all_to_all | solution.py:70
  124.0 272.3 %all-reduce.5.cloned.1.call-start = ((), (), s32[]{:S(2)}) async-start(), calls=%async_computation.4 | async-start | bytes 18874368 | tf_op jit(solution)/shard_map/psum | solution.py:199
  141.2 2.4 copy-start.17
  141.2 2.4 copy-start.49
  141.2 2.4 copy-start.54
  145.0 1.9 copy-start.36
  145.1 1.9 copy-start.38
  161.6 3.1 copy-start.15
  164.8 3.4 copy-start.5
  168.2 2.5 copy-start.71
  174.3 4.5 %copy-start.25 = (bf16[256,512]{1,0:T(8,128)(2,1)S(1)}, bf16[256,512]{1,0:T(8,128)(2,1)}, u32[]{:S(2)}) copy-start(bf16[256,512]{1,0:T(8,128)(2,1)} %copy-done.24) | copy-start | bytes 786436
  174.3 4.5 %copy-start.27 = (bf16[256,512]{1,0:T(8,128)(2,1)S(1)}, bf16[256,512]{1,0:T(8,128)(2,1)}, u32[]{:S(2)}) copy-start(bf16[256,512]{1,0:T(8,128)(2,1)} %copy-done.26) | copy-start | bytes 786436
  174.3 4.5 %copy-start.41 = (bf16[256,512]{1,0:T(8,128)(2,1)S(1)}, bf16[256,512]{1,0:T(8,128)(2,1)}, u32[]{:S(2)}) copy-start(bf16[256,512]{1,0:T(8,128)(2,1)} %param.22) | copy-start | bytes 786436
  178.8 2.3 copy-start.65
  192.0 3.2 copy-start.11
  201.0 11.7 %copy-start.23 = (bf16[256,512]{1,0:T(8,128)(2,1)S(1)}, bf16[256,512]{1,0:T(8,128)(2,1)}, u32[]{:S(2)}) copy-start(bf16[256,512]{1,0:T(8,128)(2,1)} %param.29) | copy-start | bytes 786436
  204.4 9.7 %copy-start.52 = (f32[512]{0:T(512)S(1)}, f32[512]{0:T(512)}, u32[]{:S(2)}) copy-start(f32[512]{0:T(512)} %get-tuple-element.76) | copy-start | bytes 6148
  204.4 9.7 %copy-start.51 = (f32[512]{0:T(512)S(1)}, f32[512]{0:T(512)}, u32[]{:S(2)}) copy-start(f32[512]{0:T(512)} %get-tuple-element.78) | copy-start | bytes 6148
  204.4 52.5 %copy-start.50 = (f32[512]{0:T(512)S(1)}, f32[512]{0:T(512)}, u32[]{:S(2)}) copy-start(f32[512]{0:T(512)} %get-tuple-element.72) | copy-start | bytes 6148
  208.1 49.4 %all-to-all-start.2 = ((bf16[8,4,4,512]{3,2,1,0:T(4,128)(2,1)}), bf16[8,4,4,512]{3,2,1,0:T(4,128)(2,1)S(1)}, u32[]{:S(2)}, u32[]{:S(2)}) async-start(bf16[8,4,4,512]{3,2,1,0:T(4,128)(2,1)} %convert_element_type.97), calls=%async_computation.2 | async-start | bytes 262144 | tf_op jit(solution)/shard_map/all_to_all | solution.py:169
  258.2 25.1 %all-to-all-start.3 = ((bf16[8,4,4,512]{3,2,0,1:T(4,128)(2,1)}), bf16[8,4,4,512]{3,2,0,1:T(4,128)(2,1)S(1)}, u32[]{:S(2)}, u32[]{:S(2)}) async-start(bf16[8,4,4,512]{3,2,0,1:T(4,128)(2,1)} %copy.113), calls=%async_computation.3 | async-start | bytes 262144 | tf_op jit(solution)/shard_map/all_to_all | solution.py:168
  275.5 7.7 %copy-start.20 = (f32[256,512]{1,0:T(8,128)S(1)}, f32[256,512]{1,0:T(8,128)}, u32[]{:S(2)}) copy-start(f32[256,512]{1,0:T(8,128)} %scatter_custom_fusion.2) | copy-start | bytes 1572868
  283.6 112.7 %copy-start.35 = (bf16[1024,512]{1,0:T(8,128)(2,1)S(1)}, bf16[1024,512]{1,0:T(8,128)(2,1)}, u32[]{:S(2)}) copy-start(bf16[1024,512]{1,0:T(8,128)(2,1)} %copy-done.34) | copy-start | bytes 3145732
  285.1 115.0 %copy-start.6 = (f32[256,512]{1,0:T(8,128)}, f32[256,512]{1,0:T(8,128)S(1)}, u32[]{:S(2)}) copy-start(f32[256,512]{1,0:T(8,128)S(1)} %scatter_fusion) | copy-start | bytes 1572868
  396.3 3.8 copy-start.10
  396.3 3.8 copy-start.21
  396.3 3.8 copy-start.55
  396.3 3.8 copy-start.64
  400.1 2.6 copy-start.8
  400.1 3.1 copy-start.14
  400.1 3.9 copy-start.19
  404.1 1.9 copy-start.31
  404.1 3.0 copy-start.18
  (29 other events, 38.1 us)
Sparse Core Ops, SparseCore 0:
  200.4 195.8 all-reduce.4
where the time goes:
time: 421 us; the launch traced here: 416 us
  waiting for transfers between devices  111 us (26%)
  blocking collectives  105 us (25%)
  local copies, waits for them, and re-layouts  64.5 us (15%)
  other arithmetic  60 us (14%)
  matrix products  41.4 us (10%)
  starting transfers between devices  19.3 us (5%)
  between operations  15.2 us (4%)
    psum x1, waiting for transfers between devices, per_device(): lax.psum((node_first_total, node_second_total, node_gain_total, coarse_lo...  111 us
    psum x1, blocking collectives, per_device(): lax.psum(jnp.dot(onehot_rows, new_ups, preferred_element_type=jnp.float32...  61.8 us
    psum x1, blocking collectives, per_device(): lax.psum((node_first_total, node_second_total, node_gain_total, coarse_lo...  42.8 us
    unnamed x149, local copies, waits for them, and re-layouts  19.4 us
    scatter-add x1, other arithmetic, per_device(): jax.ops.segment_sum(edge_grad_inputs[:, latent_width:2 * latent_width], e...  9.1 us
    dot_general x4, matrix products, mlp_backward(): grad_first = jnp.dot(inputs.T, grad_pre, preferred_element_type=jnp.float32)  8.44 us
  transfers between devices with their start and end apart: 5, of which 1 were waited for; matrix products, arithmetic and copies ran while one was open for 18% of the time, Pallas kernels for 0%

commit v1 on v0

--- a/solution.py
+++ b/solution.py
@@ -119,8 +119,11 @@
     )
     row_ids = jnp.arange(coarse_count, dtype=jnp.int32)
     onehot_rows = (row_ids[:, None] == up_receiver[None, :]).astype(jnp.bfloat16)
-    coarse_total = lax.psum(
-        jnp.dot(onehot_rows, new_ups, preferred_element_type=jnp.float32), ("face", "band")
+    coarse_total = jnp.sum(
+        lax.all_gather(
+            jnp.dot(onehot_rows, new_ups, preferred_element_type=jnp.float32), ("face", "band")
+        ),
+        axis=0,
     )
     coarse_inputs = jnp.concatenate([coarse_latents, coarse_total.astype(jnp.bfloat16)], 1)
     unused_coarse, coarse_cache = mlp_forward(

time: 421 us -> 658 us (1.56)
  waiting for transfers between devices: 111 us -> 384 us
  blocking collectives: 105 us -> 39.7 us
  other arithmetic: 60 us -> 82.9 us
    all_gather x0 -> x1, waiting for transfers between devices: none -> 268 us  [per_device(): lax.all_gather(jnp.dot(onehot_rows, new_ups, preferred_element_type=jnp.f...]
    psum x1 -> x0, blocking collectives: 61.8 us -> none  [per_device(): lax.psum(jnp.dot(onehot_rows, new_ups, preferred_element_type=jnp.float32...]
    reduce_sum x0 -> x1, other arithmetic: none -> 22.1 us  [per_device(): jnp.sum(lax.all_gather(jnp.dot(onehot_rows, new_ups, preferred_element_ty...]
    psum x1, waiting for transfers between devices: 111 us -> 99.4 us  [per_device(): lax.psum((node_first_total, node_second_total, node_gain_total, coarse_lo...]
    all_to_all x1, waiting for transfers between devices: 0.01 us -> 9.21 us  [per_device(): lax.all_to_all(sectioned_back.astype(jnp.bfloat16), 'face', split_axis=0,...]
    all_to_all x1, waiting for transfers between devices: 0.01 us -> 7.39 us  [per_device(): lax.all_to_all(sectioned, 'face', split_axis=0, concat_axis=0, tiled=True)]
    unnamed x149 -> x157, local copies, waits for them, and re-layouts: 19.4 us -> 24.2 us
  transfers between devices with their start and end apart: 5 -> 6, of which waited for: 1 -> 4; matrix products, arithmetic and copies ran while one was open for 18% -> 16% of each run, Pallas kernels for 0% -> 0%
where the time goes in v1:
time: 658 us; the launch traced here: 653 us
  waiting for transfers between devices  384 us (58%)
  other arithmetic  82.9 us (13%)
  local copies, waits for them, and re-layouts  70.5 us (11%)
  matrix products  42.6 us (6%)
  blocking collectives  39.7 us (6%)
  starting transfers between devices  18 us (3%)
  between operations  15.2 us (2%)
    all_gather x1, waiting for transfers between devices, per_device(): lax.all_gather(jnp.dot(onehot_rows, new_ups, preferred_element_type=jnp.f...  268 us
    psum x1, waiting for transfers between devices, per_device(): lax.psum((node_first_total, node_second_total, node_gain_total, coarse_lo...  99.4 us
    psum x1, blocking collectives, per_device(): lax.psum((node_first_total, node_second_total, node_gain_total, coarse_lo...  39.7 us
    unnamed x157, local copies, waits for them, and re-layouts  24.2 us
    reduce_sum x1, other arithmetic, per_device(): jnp.sum(lax.all_gather(jnp.dot(onehot_rows, new_ups, preferred_element_ty...  22.1 us
  transfers between devices with their start and end apart: 6, of which 4 were waited for; matrix products, arithmetic and copies ran while one was open for 16% of the time, Pallas kernels for 0%

profile of v1, /device:TPU:0, one launch (start us, length us, event | category | flops | bytes accessed | tf_op | source)
XLA Modules:
  0.0 652.5 jit_solution(7456087467410346280)
XLA Ops:
  10.1 2.6 gather_fusion.5
  16.5 1.9 fusion.22
  20.6 7.3 %all-to-all-start = ((bf16[8,4,4,512]{3,2,1,0:T(4,128)(2,1)}), bf16[8,4,4,512]{3,2,1,0:T(4,128)(2,1)S(1)}, u32[]{:S(2)}, u32[]{:S(2)}) async-start(bf16[8,4,4,512]{3,2,1,0:T(4,128)(2,1)} %broadcast_select_fusion.4), calls=%async_computation | async-start | bytes 262144 | tf_op jit(solution)/shard_map/all_to_all | solution.py:71
  28.0 7.4 %all-to-all-done = bf16[8,4,4,512]{3,2,1,0:T(4,128)(2,1)S(1)} async-done(((bf16[8,4,4,512]{3,2,1,0:T(4,128)(2,1)}), bf16[8,4,4,512]{3,2,1,0:T(4,128)(2,1)S(1)}, u32[]{:S(2)}, u32[]{:S(2)}) %all-to-all-start) | async-done | bytes 131104 | tf_op jit(solution)/shard_map/all_to_all | solution.py:71
  36.0 3.3 all-to-all-start.1
  39.7 4.0 gather_fusion.2
  45.0 2.4 copy.101
  50.1 5.1 gather_fusion.1
  55.2 2.4 copy.106
  59.1 1.8 fusion.17
  68.4 4.9 gather_fusion.3
  73.3 3.5 copy.110
  76.8 3.3 multiply_reduce_fusion
  84.0 5.4 fusion.68
  89.3 9.1 %scatter_custom_fusion = f32[1408,512]{1,0:T(8,128)} fusion(s32[1024]{0:T(1024)S(1)} %copy-done.53, f32[1024,1536]{1,0:T(8,128)} %fusion.68, f32[]{:T(128)} %constant.129.clone.1), kind=kCustom, calls=%fused_computation.28 | custom fusion | flops 524288 | bytes 4981248 | tf_op jit(solution)/shard_map/scatter-add | solution.py:161
  98.5 3.1 slice.75
  101.6 2.0 fusion.38
  105.9 3.5 fusion.16
  109.3 267.7 %all-gather.3.cloned.1.call-done = f32[32768,512]{1,0:T(8,128)} async-done(((f32[1024,512]{1,0:T(8,128)}), f32[32768,512]{1,0:T(8,128)}) %all-gather.3.cloned.1.call-update) | async-done | bytes 67108880 | tf_op jit(solution)/shard_map/all_gather | solution.py:123
  377.0 22.1 %reduce_sum.199 = bf16[1024,512]{1,0:T(8,128)(2,1)} reduce(f32[32,1024,512]{2,1,0:T(8,128)} %bitcast.1, f32[]{:T(128)} %constant.129.clone.1), dimensions={0}, to_apply=%region_12.13 | reduce | flops 16252928 | bytes 68157440 | tf_op jit(solution)/shard_map/reduce_sum | solution.py:122
  399.2 2.8 fusion.15
  402.0 2.2 fusion.66
  404.2 3.0 copy.111
  407.2 2.1 multiply_reduce_fusion.1
  415.0 1.9 copy-done.13
  418.5 3.7 gather_fusion.6
  422.2 2.0 multiply_reduce_fusion.5
  427.4 1.8 convolution_add_fusion.2
  429.2 1.9 fusion.70
  431.6 2.3 convolution_add_fusion
  433.9 5.5 scatter_custom_fusion.4
  441.1 3.5 all-to-all-start.2
  445.2 9.2 %all-to-all-done.2 = bf16[8,4,4,512]{3,2,1,0:T(4,128)(2,1)S(1)} async-done(((bf16[8,4,4,512]{3,2,1,0:T(4,128)(2,1)}), bf16[8,4,4,512]{3,2,1,0:T(4,128)(2,1)S(1)}, u32[]{:S(2)}, u32[]{:S(2)}) %all-to-all-start.2) | async-done | bytes 131104 | tf_op jit(solution)/shard_map/all_to_all | solution.py:172
  455.2 3.5 all-to-all-start.3
  460.0 3.1 slice.78
  463.1 3.0 copy.118
  466.1 4.2 add.238
  470.4 2.9 copy.117
  473.2 7.6 %scatter_custom_fusion.1 = f32[256,512]{1,0:T(8,128)S(1)} fusion(f32[256,512]{1,0:T(8,128)S(1)} %fusion.30, s32[1024]{0:T(1024)S(1)} %copy-done.54, f32[1024,1536]{1,0:T(8,128)} %fusion.68), kind=kCustom, calls=%fused_computation.26 | custom fusion | flops 524288 | bytes 2621440 | tf_op jit(solution)/shard_map/scatter-add | solution.py:184
  482.9 3.4 scatter_custom_fusion.2
  487.6 1.7 scatter_fusion
  489.3 39.7 %all-reduce = (f32[512]{0:T(512)S(1)}, f32[512]{0:T(512)S(1)}) all-reduce(f32[512]{0:T(512)S(1)} %add.242, f32[512]{0:T(512)S(1)} %get-tuple-element.78), channel_id=1, replica_groups=mesh['face'=8,'band'=4] {'face','band'}, use_global_device_ids=true, to_apply=%region_27.28 | all-reduce | flops 1024 | bytes 8192 | tf_op jit(solution)/shard_map/psum | solution.py:202
  530.1 2.1 slice_add_fusion
  532.2 99.4 %all-reduce.4.cloned.1.call-done = (f32[1024,512]{1,0:T(8,128)}, f32[1536,512]{1,0:T(8,128)}, f32[512,512]{1,0:T(8,128)}, f32[1024,512]{1,0:T(8,128)}, f32[512,512]{1,0:T(8,128)}) async-done(((f32[1024,512]{1,0:T(8,128)}, f32[1536,512]{1,0:T(8,128)}, f32[512,512]{1,0:T(8,128)}, f32[1024,512]{1,0:T(8,128)}, f32[512,512]{1,0:T(8,128)}), (f32[1024,512]{1,0:T(8,128)}, f32[1536,512]{1,0:T(8,128)}, ...) | async-done | bytes 9437200 | tf_op jit(solution)/shard_map/psum | solution.py:202
  631.7 4.1 fusion.14
  635.8 2.6 add_multiply_fusion
  638.4 2.0 broadcast_multiply_fusion
  642.4 2.0 fusion.7
  (240 shorter events, 51.6 us)
Async XLA Ops:
  7.2 7.0 %copy-start = (bf16[1536,512]{1,0:T(8,128)(2,1)S(1)}, bf16[1536,512]{1,0:T(8,128)(2,1)}, u32[]{:S(2)}) copy-start(bf16[1536,512]{1,0:T(8,128)(2,1)} %param.23) | copy-start | bytes 4718596
  7.2 5.7 copy-start.1
  7.2 369.8 %all-gather.3.cloned.1.call-start = ((), (), s32[]{:S(2)}) async-start(), calls=%async_computation.4 | async-start | bytes 69206016 | tf_op jit(solution)/shard_map/all_gather | solution.py:123
  16.5 1.9 copy-start.52
  18.4 9.5 %copy-start.54 = (s32[1024]{0:T(1024)S(1)}, s32[1024]{0:T(1024)}, u32[]{:S(2)}) copy-start(s32[1024]{0:T(1024)} %param.35) | copy-start | bytes 12292
  18.4 9.5 %copy-start.53 = (s32[1024]{0:T(1024)S(1)}, s32[1024]{0:T(1024)}, u32[]{:S(2)}) copy-start(s32[1024]{0:T(1024)} %param.34) | copy-start | bytes 12292
  20.6 14.7 %all-to-all-start = ((bf16[8,4,4,512]{3,2,1,0:T(4,128)(2,1)}), bf16[8,4,4,512]{3,2,1,0:T(4,128)(2,1)S(1)}, u32[]{:S(2)}, u32[]{:S(2)}) async-start(bf16[8,4,4,512]{3,2,1,0:T(4,128)(2,1)} %broadcast_select_fusion.4), calls=%async_computation | async-start | bytes 262144 | tf_op jit(solution)/shard_map/all_to_all | solution.py:71
  36.0 12.6 %all-to-all-start.1 = ((bf16[8,4,4,512]{3,2,0,1:T(4,128)(2,1)}), bf16[8,4,4,512]{3,2,0,1:T(4,128)(2,1)S(1)}, u32[]{:S(2)}, u32[]{:S(2)}) async-start(bf16[8,4,4,512]{3,2,0,1:T(4,128)(2,1)} %copy.104), calls=%async_computation.1 | async-start | bytes 262144 | tf_op jit(solution)/shard_map/all_to_all | solution.py:70
  39.4 592.3 %all-reduce.4.cloned.1.call-start = ((), (), s32[]{:S(2)}) async-start(), calls=%async_computation.5 | async-start | bytes 18874368 | tf_op jit(solution)/shard_map/psum | solution.py:202
  45.0 2.4 copy-start.32
  55.2 2.4 copy-start.17
  62.6 2.1 copy-start.58
  73.3 3.5 copy-start.15
  76.8 3.4 copy-start.5
  80.2 2.5 copy-start.74
  98.5 3.2 copy-start.46
  98.5 3.2 copy-start.49
  101.6 2.0 copy-start.26
  101.6 2.0 copy-start.68
  103.6 2.3 copy-start.42
  377.0 22.2 %copy-start.8 = (bf16[1024,512]{1,0:T(8,128)(2,1)S(1)}, bf16[1024,512]{1,0:T(8,128)(2,1)}, u32[]{:S(2)}) copy-start(bf16[1024,512]{1,0:T(8,128)(2,1)} %param.20) | copy-start | bytes 3145732
  399.2 2.8 copy-start.59
  402.0 2.2 copy-start.71
  404.2 5.1 copy-start.7
  407.2 2.2 copy-start.2
  410.6 1.9 copy-start.60
  415.0 2.0 copy-start.13
  418.5 3.7 copy-start.11
  418.5 3.7 copy-start.47
  422.2 2.8 copy-start.70
  427.4 3.6 copy-start.31
  427.4 3.6 copy-start.44
  429.1 2.5 copy-start.18
  429.2 2.5 copy-start.29
  439.3 19.4 %copy-start.27 = (bf16[256,512]{1,0:T(8,128)(2,1)S(1)}, bf16[256,512]{1,0:T(8,128)(2,1)}, u32[]{:S(2)}) copy-start(bf16[256,512]{1,0:T(8,128)(2,1)} %param.29) | copy-start | bytes 786436
  441.1 13.4 %all-to-all-start.2 = ((bf16[8,4,4,512]{3,2,1,0:T(4,128)(2,1)}), bf16[8,4,4,512]{3,2,1,0:T(4,128)(2,1)S(1)}, u32[]{:S(2)}, u32[]{:S(2)}) async-start(bf16[8,4,4,512]{3,2,1,0:T(4,128)(2,1)} %convert_element_type.97), calls=%async_computation.2 | async-start | bytes 262144 | tf_op jit(solution)/shard_map/all_to_all | solution.py:172
  455.2 25.7 %all-to-all-start.3 = ((bf16[8,4,4,512]{3,2,0,1:T(4,128)(2,1)}), bf16[8,4,4,512]{3,2,0,1:T(4,128)(2,1)S(1)}, u32[]{:S(2)}, u32[]{:S(2)}) async-start(bf16[8,4,4,512]{3,2,0,1:T(4,128)(2,1)} %copy.113), calls=%async_computation.3 | async-start | bytes 262144 | tf_op jit(solution)/shard_map/all_to_all | solution.py:171
  480.9 5.4 copy-start.21
  480.9 5.4 copy-start.55
  489.3 146.4 %copy-start.6 = (f32[256,512]{1,0:T(8,128)}, f32[256,512]{1,0:T(8,128)S(1)}, u32[]{:S(2)}) copy-start(f32[256,512]{1,0:T(8,128)S(1)} %scatter_fusion) | copy-start | bytes 1572868
  631.7 4.1 copy-start.9
  631.7 4.1 copy-start.22
  631.7 4.1 copy-start.57
  631.7 4.1 copy-start.66
  635.8 2.6 copy-start.19
  638.4 3.3 copy-start.14
  638.4 4.0 copy-start.20
  642.4 2.0 copy-start.35
  (34 other events, 45.7 us)
Sparse Core Ops, SparseCore 0:
  18.6 358.3 all-gather.2
  439.5 192.1 all-reduce.3
